TPU v7x, 256 devices: a whole 4x4x8 slice. The times are simulated.
256 devices in a mesh: tok: 8 (over z), tp: 16 (over y, x), grp: 2 (over core).
Axes of the slice: x: 4, y: 4, z: 8, core: 2. Of those that a mesh axis runs over, the one named last changes fastest.
Arguments:
- hidden: bfloat16 [2048, 6144], P(('tok', 'grp'), 'tp'), may hold values from -6 to 6
- gain: bfloat16 [6144], P('tp'), may hold values from 0.5 to 1.5
- expert_ids: int32 [2048, 2], P(('tok', 'grp')), may hold values from 0 to 7, all different within a row; in each aligned block of 128 rows (0 to 127, 128 to 255, ...) at most 40 rows name the same one
- gate_weights: float32 [2048, 2], P(('tok', 'grp')), may hold values from 0.1 to 0.9
- segment_ids: int32 [2048], P(('tok', 'grp')), may hold values from 0 to 15, never falling along the last dimension, each value on 1 to 384 neighbouring positions
- upstream: bfloat16 [2048, 6144], P(('tok', 'grp'), 'tp'), may hold values from -6 to 6
- w_gate: bfloat16 [8, 6144, 8192], P('tok', None, ('tp', 'grp')), may hold values from -0.078125 to 0.078125
- w_up: bfloat16 [8, 6144, 8192], P('tok', None, ('tp', 'grp')), may hold values from -0.078125 to 0.078125
- w_down: bfloat16 [8, 8192, 6144], P('tok', ('tp', 'grp')), may hold values from -0.0625 to 0.0625
Outputs:
- mixed: bfloat16 [2048, 6144], P(('tok', 'grp'), 'tp')
- importance: float32 [8, 8192], P('tok', ('tp', 'grp'))
Inputs may be any that keep to these rules, and one draw needn't show every extreme that they name: `expert_ids`: each token names 2 different experts. Within the tokens of one token shard (aligned blocks of 128 rows) no expert is named by more than 40 tokens, and in some block one expert is named by exactly 40. `segment_ids`: never falling along the tokens; every document holds between 1 and 384 tokens.
All inputs are finite; a program needn't handle non-finite values.
Results may differ from a plain program's by a relative error of at most 0.0095.
Values may be sent and summed in bfloat16 or wider, within the bound.
No kernel may reach another device: no remote copies, remote signals or barrier semaphores. Data moves between devices by JAX's collectives and lax.ppermute only.
A program may use at most 128 MiB of HBM per device.

v0:
```python
import jax
import jax.numpy as jnp
from jax import lax
from jax.sharding import PartitionSpec as P


def expert_pass(rows_in, cot_in, gate_mat, up_mat, down_mat):
    gate_pre = jnp.dot(rows_in, gate_mat, preferred_element_type=jnp.float32)
    up_proj = jnp.dot(rows_in, up_mat, preferred_element_type=jnp.float32)
    sigmoid_gate = jax.nn.sigmoid(gate_pre)
    activated = gate_pre * sigmoid_gate
    hidden_act = (activated * up_proj).astype(jnp.bfloat16)
    grad_act = lax.dot_general(
        cot_in, down_mat, (((1,), (1,)), ((), ())), preferred_element_type=jnp.float32
    )
    grad_gate = (
        grad_act * up_proj * sigmoid_gate * (1.0 + gate_pre * (1.0 - sigmoid_gate))
    ).astype(jnp.bfloat16)
    grad_up = (grad_act * activated).astype(jnp.bfloat16)
    grad_wgate = lax.dot_general(
        rows_in, grad_gate, (((0,), (0,)), ((), ())), preferred_element_type=jnp.float32
    )
    grad_wup = lax.dot_general(
        rows_in, grad_up, (((0,), (0,)), ((), ())), preferred_element_type=jnp.float32
    )
    grad_wdown = lax.dot_general(
        hidden_act, cot_in, (((0,), (0,)), ((), ())), preferred_element_type=jnp.float32
    )
    scores = jnp.sum(jnp.abs(grad_wgate * gate_mat.astype(jnp.float32)), axis=0)
    scores = scores + jnp.sum(jnp.abs(grad_wup * up_mat.astype(jnp.float32)), axis=0)
    scores = scores + jnp.sum(jnp.abs(grad_wdown * down_mat.astype(jnp.float32)), axis=1)
    return (hidden_act, scores)


def on_device(hidden, gain, expert_ids, gate_weights, segment_ids, upstream, w_gate, w_up, w_down):
    rows_here = hidden.shape[0]
    top_count = expert_ids.shape[1]
    experts = lax.axis_size("tok")
    groups = lax.axis_size("grp")
    capacity = 5 * rows_here // (2 * experts)
    width = w_gate.shape[1]
    documents = jnp.arange(experts * groups, dtype=jnp.int32)
    doc_onehot = (segment_ids[:, None] == documents[None, :]).astype(jnp.float32)
    doc_len = lax.psum(jnp.sum(doc_onehot, axis=0), ("tok", "grp"))
    tok_len = jnp.sum(doc_onehot * doc_len[None, :], axis=1)
    tok_weight = rows_here / tok_len
    onehot = (
        expert_ids.reshape(-1)[:, None] == jnp.arange(experts, dtype=jnp.int32)[None, :]
    ).astype(jnp.int32)
    before = jnp.cumsum(onehot, axis=0) - onehot
    slot_ids = jnp.sum(before * onehot, axis=1).reshape(rows_here, top_count)
    targets = expert_ids * capacity + slot_ids
    all_slots = jnp.arange(experts * capacity, dtype=jnp.int32)
    matches = all_slots[:, None, None] == targets[None, :, :]
    placing = jnp.any(matches, axis=2).astype(jnp.bfloat16)
    scaled = gate_weights * tok_weight[:, None]
    slot_scale = jnp.sum(jnp.where(matches, scaled[None, :, :], 0.0), axis=(1, 2))
    combining = jnp.sum(jnp.where(matches, gate_weights[None, :, :], 0.0), axis=2)
    wide_hidden = hidden.astype(jnp.float32)
    squares = lax.psum(jnp.sum(wide_hidden * wide_hidden, axis=1), "tp")
    scaling = lax.rsqrt(squares / width + 1e-05)
    normed = (wide_hidden * scaling[:, None] * gain.astype(jnp.float32)[None, :]).astype(
        jnp.bfloat16
    )
    block_rows = jnp.dot(placing, normed, preferred_element_type=jnp.float32).astype(jnp.bfloat16)
    block_cot = jnp.dot(placing, upstream, preferred_element_type=jnp.float32) * slot_scale[:, None]
    block_rows = block_rows.reshape(experts, capacity, -1)
    block_cot = block_cot.astype(jnp.bfloat16).reshape(experts, capacity, -1)
    came_rows, came_cot = (
        lax.all_to_all(block_rows, "tok", split_axis=0, concat_axis=0, tiled=True),
        lax.all_to_all(block_cot, "tok", split_axis=0, concat_axis=0, tiled=True),
    )
    part_rows, part_cot = (
        lax.all_gather(came_rows, "tp", axis=2, tiled=True),
        lax.all_gather(came_cot, "tp", axis=2, tiled=True),
    )
    pooled_rows, pooled_cot = (
        lax.all_gather(part_rows, "grp", axis=0, tiled=True),
        lax.all_gather(part_cot, "grp", axis=0, tiled=True),
    )
    rows_in = pooled_rows.reshape(-1, width)
    cot_in = pooled_cot.reshape(-1, width)
    gate_mat = w_gate[0]
    up_mat = w_up[0]
    down_mat = w_down[0]
    hidden_act, scores = expert_pass(rows_in, cot_in, gate_mat, up_mat, down_mat)
    importance = scores / (rows_here * experts * groups)
    partial_value = lax.psum_scatter(
        lax.dot_general(
            down_mat, hidden_act, (((0,), (1,)), ((), ())), preferred_element_type=jnp.float32
        ).astype(jnp.bfloat16),
        "tp",
        scatter_dimension=0,
        tiled=True,
    )
    summed = lax.psum_scatter(partial_value, "grp", scatter_dimension=1, tiled=True).astype(
        jnp.float32
    )
    slice_width = summed.shape[0]
    outgoing = summed.astype(jnp.bfloat16).reshape(slice_width, experts, capacity)
    returned = lax.all_to_all(outgoing, "tok", split_axis=1, concat_axis=1, tiled=True)
    returned = returned.reshape(slice_width, experts * capacity).astype(jnp.float32)
    combined = lax.dot_general(
        combining,
        returned,
        (((0,), (1,)), ((), ())),
        precision=lax.Precision.HIGHEST,
        preferred_element_type=jnp.float32,
    )
    mixed = (hidden.astype(jnp.float32) + combined).astype(jnp.bfloat16)
    return (mixed, importance[None, :])


def solution(mesh):
    placed = (
        P(("tok", "grp"), "tp"),
        P("tp"),
        P(("tok", "grp"), None),
        P(("tok", "grp"), None),
        P(("tok", "grp")),
        P(("tok", "grp"), "tp"),
        P("tok", None, ("tp", "grp")),
        P("tok", None, ("tp", "grp")),
        P("tok", ("tp", "grp"), None),
    )
    return jax.shard_map(
        on_device,
        mesh=mesh,
        in_specs=placed,
        out_specs=(P(("tok", "grp"), "tp"), P("tok", ("tp", "grp"))),
        check_vma=False,
    )
```

profile of v0, /device:TPU:1, one launch (start us, length us, event | category | flops | bytes accessed | tf_op | source)
XLA Modules:
  0.0 378.7 jit_solution(2218602018310981666)
XLA Ops:
  7.2 0.9 copy.31
  8.2 0.1 eq.56
  8.3 0.1 eq.52
  8.5 1.0 fusion.19
  9.5 34.2 %psum.14 = f32[128]{0:T(128)S(1)} all-reduce(f32[128]{0:T(128)S(1)} %fusion.19), channel_id=1, replica_groups=mesh['tok'=8,'tp'=16,'grp'=2] {'tp'}, use_global_device_ids=true, to_apply=%region_6.7 | all-reduce | flops 128 | bytes 1024 | tf_op jit(solution)/shard_map/psum | solution.py:60
  43.7 0.7 convert_element_type.60
  44.4 0.6 reduce-window.6
  45.0 0.2 slice_reduce_fusion
  45.2 0.1 fusion.27
  45.3 0.1 reshape.79
  45.5 0.1 copy.33
  45.5 0.7 multiply_add_fusion
  46.3 1.2 convolution_convert_fusion.1
  47.5 17.2 %all_to_all.15 = bf16[8,40,384]{2,1,0:T(8,128)(2,1)} all-to-all(bf16[8,40,384]{2,1,0:T(8,128)(2,1)S(1)} %bitcast.56), channel_id=1, replica_groups=mesh['tok'=8,'tp'=16,'grp'=2] {'tok'}, dimensions={0} | all-to-all | bytes 491520 | tf_op jit(solution)/shard_map/all_to_all | solution.py:70
  64.7 0.0 all-gather.9.cloned.1.call-start
  64.8 0.8 convert_reduce_fusion
  65.6 32.2 %psum.15 = f32[16]{0:T(128)S(1)} all-reduce(f32[16]{0:T(128)S(1)} %convert_reduce_fusion), channel_id=1, replica_groups=mesh['tok'=8,'tp'=16,'grp'=2] {'tok','grp'}, use_global_device_ids=true, to_apply=%region_10.11 | all-reduce | flops 16 | bytes 128 | tf_op jit(solution)/shard_map/psum | solution.py:44
  97.8 0.7 select_reduce_fusion.2
  98.5 0.7 broadcast_multiply_fusion
  99.2 1.5 select_reduce_fusion
  100.7 0.2 fusion.14
  101.0 12.8 %all_to_all.16 = bf16[8,40,384]{2,1,0:T(8,128)(2,1)} all-to-all(bf16[8,40,384]{2,1,0:T(8,128)(2,1)S(1)} %bitcast.57), channel_id=1, replica_groups=mesh['tok'=8,'tp'=16,'grp'=2] {'tok'}, dimensions={0} | all-to-all | bytes 491520 | tf_op jit(solution)/shard_map/all_to_all | solution.py:71
  113.8 0.0 all-gather.7.cloned.1.call-start
  113.8 10.2 %all-gather.5.cloned.1.call-done = bf16[8,40,6144]{2,1,0:T(8,128)(2,1)} async-done(((bf16[8,40,384]{2,1,0:T(8,128)(2,1)}), bf16[8,40,6144]{2,1,0:T(8,128)(2,1)}) %all-gather.5.cloned.1.call-update) | async-done | bytes 3932176 | tf_op jit(solution)/shard_map/all_gather | solution.py:74
  124.1 0.0 all-gather.11.cloned.1.call-start
  124.1 62.4 %all-gather.9.cloned.1.call-done = bf16[8,40,6144]{2,1,0:T(8,128)(2,1)} async-done(((bf16[8,40,384]{2,1,0:T(8,128)(2,1)}), bf16[8,40,6144]{2,1,0:T(8,128)(2,1)}) %all-gather.9.cloned.1.call-update) | async-done | bytes 3932176 | tf_op jit(solution)/shard_map/all_gather | solution.py:75
  186.5 0.0 reduce-scatter.7.cloned.1.call-start
  186.5 27.7 %all-gather.7.cloned.1.call-done = bf16[16,40,6144]{2,1,0:T(8,128)(2,1)} async-done(((bf16[8,40,6144]{2,1,0:T(8,128)(2,1)}), bf16[16,40,6144]{2,1,0:T(8,128)(2,1)}) %all-gather.7.cloned.1.call-update) | async-done | bytes 7864336 | tf_op jit(solution)/shard_map/all_gather | solution.py:78
  214.2 5.6 %fusion.9 = f32[640,256]{1,0:T(8,128)S(1)} fusion(bf16[640,6144]{1,0:T(8,128)(2,1)} %bitcast.60, bf16[1,6144,256]{2,1,0:T(8,128)(2,1)S(1)} %copy-done.4), kind=kOutput, calls=%fused_computation.13 | convolution fusion | flops 2013265920 | bytes 11665408 | tf_op jit(solution)/shard_map/dot_general | solution.py:8
  219.8 0.8 copy-done.6
  220.6 3.0 multiply_convert_fusion.2
  223.6 0.7 copy-done.2
  224.4 6.1 %fusion = bf16[6144,640]{0,1:T(8,128)(2,1)} fusion(bf16[640,256]{1,0:T(8,128)(2,1)S(1)} %get-tuple-element.4, bf16[1,256,6144]{2,1,0:T(8,128)(2,1)S(1)} %copy-done.1), kind=kOutput, calls=%fused_computation.1 | convolution fusion | flops 2017198080 | bytes 11337728 | tf_op jit(solution)/shard_map/dot_general | solution.py:89
  230.5 10.7 %copy.34 = bf16[6144,640]{1,0:T(8,128)(2,1)} copy(bf16[6144,640]{0,1:T(8,128)(2,1)} %fusion) | data formatting | bytes 15728640
  241.2 0.2 reduce-scatter.5.cloned.1.call-start
  241.5 0.1 all-gather.11.cloned.1.call-done
  241.6 5.6 %fusion.4 = f32[640,256]{1,0:T(8,128)S(1)} fusion(bf16[640,6144]{1,0:T(8,128)(2,1)} %bitcast.53, bf16[1,256,6144]{2,1,0:T(8,128)(2,1)S(1)} %copy-done.1), kind=kOutput, calls=%fused_computation.8 | convolution fusion | flops 2013265920 | bytes 11665408 | tf_op jit(solution)/shard_map/dot_general | solution.py:13
  247.2 0.8 copy-done.9
  248.1 6.2 %fusion.11 = f32[256]{0:T(256)S(1)} fusion(bf16[1,6144,256]{2,1,0:T(8,128)(2,1)S(1)} %copy-done.5, bf16[640,6144]{1,0:T(8,128)(2,1)} %bitcast.61, f32[640,256]{1,0:T(8,128)S(1)} %copy-done.8, f32[640,256]{1,0:T(8,128)S(1)} %fusion.4, f32[640,256]{1,0:T(8,128)S(1)} %copy-done.10), kind=kOutput, calls=%fused_computation.15 | convolution fusion | flops 2021195520 | bytes 12977152 | tf_op jit(solution)/shard_map/dot_general | solution.py:20
  254.3 80.1 %reduce-scatter.7.cloned.1.call-done = bf16[384,640]{1,0:T(8,128)(2,1)} async-done(((bf16[6144,640]{1,0:T(8,128)(2,1)}), bf16[384,640]{1,0:T(8,128)(2,1)}) %reduce-scatter.7.cloned.1.call-update) | async-done | bytes 491536
  334.4 2.0 copy.35
  336.5 7.4 %fusion.12 = f32[256]{0:T(256)S(1)} fusion(bf16[1,6144,256]{2,1,0:T(8,128)(2,1)} %param.16, bf16[640,6144]{1,0:T(8,128)(2,1)} %bitcast.62, f32[640,256]{1,0:T(8,128)} %copy-done.9, f32[640,256]{1,0:T(8,128)} %copy-done.7), kind=kOutput, calls=%fused_computation.16 | convolution fusion | flops 2020540160 | bytes 12321792 | tf_op jit(solution)/shard_map/dot_general | solution.py:23
  343.8 7.7 %reduce-scatter.5.cloned.1.call-done = bf16[384,320]{0,1:T(8,128)(2,1)} async-done(((bf16[384,640]{0,1:T(8,128)(2,1)}), bf16[384,320]{0,1:T(8,128)(2,1)}) %reduce-scatter.5.cloned.1.call-update) | async-done | bytes 245776 | tf_op jit(solution)/shard_map/reduce_scatter | solution.py:96
  351.5 6.5 %all-to-all-start.1 = ((bf16[384,8,40]{0,2,1:T(8,128)(2,1)}), bf16[384,8,40]{0,2,1:T(8,128)(2,1)S(1)}, u32[]{:S(2)}, u32[]{:S(2)}) async-start(bf16[384,8,40]{0,2,1:T(8,128)(2,1)} %bitcast.58), calls=%async_computation.2 | async-start | bytes 491520 | tf_op jit(solution)/shard_map/all_to_all | solution.py:101
  358.0 6.5 %fusion.13 = f32[256]{0:T(256)S(1)} fusion(bf16[1,256,6144]{2,1,0:T(8,128)(2,1)S(1)} %copy-done.1, bf16[640,256]{1,0:T(8,128)(2,1)} %copy-done.2, bf16[640,6144]{1,0:T(8,128)(2,1)} %bitcast.54), kind=kOutput, calls=%fused_computation.17 | convolution fusion | flops 2019557120 | bytes 11338752 | tf_op jit(solution)/shard_map/dot_general | solution.py:26
  364.5 0.6 add_multiply_fusion
  365.0 4.8 %all-to-all-done.1 = bf16[384,8,40]{0,2,1:T(8,128)(2,1)S(1)} async-done(((bf16[384,8,40]{0,2,1:T(8,128)(2,1)}), bf16[384,8,40]{0,2,1:T(8,128)(2,1)S(1)}, u32[]{:S(2)}, u32[]{:S(2)}) %all-to-all-start.1) | async-done | bytes 245792 | tf_op jit(solution)/shard_map/all_to_all | solution.py:101
  369.8 2.0 fusion.15
  (32 shorter events, 0.3 us)
Async XLA Ops:
  7.2 93.6 %copy-start = (bf16[128,384]{1,0:T(8,128)(2,1)S(1)}, bf16[128,384]{1,0:T(8,128)(2,1)}, u32[]{:S(2)}) copy-start(bf16[128,384]{1,0:T(8,128)(2,1)} %param.14) | copy-start | bytes 294916
  7.2 207.0 %copy-start.4 = (bf16[1,6144,256]{2,1,0:T(8,128)(2,1)S(1)}, bf16[1,6144,256]{2,1,0:T(8,128)(2,1)}, u32[]{:S(2)}) copy-start(bf16[1,6144,256]{2,1,0:T(8,128)(2,1)} %param.15) | copy-start | bytes 9437188
  7.2 116.8 %all-gather.5.cloned.1.call-start = ((), (), s32[]{:S(2)}) async-start(), calls=%async_computation.5 | async-start | bytes 4177920 | tf_op jit(solution)/shard_map/all_gather | solution.py:74
  64.7 121.7 %all-gather.9.cloned.1.call-start = ((), (), s32[]{:S(2)}) async-start(), calls=%async_computation.8 | async-start | bytes 4177920 | tf_op jit(solution)/shard_map/all_gather | solution.py:75
  113.8 100.4 %all-gather.7.cloned.1.call-start = ((), (), s32[]{:S(2)}) async-start(), calls=%async_computation.6 | async-start | bytes 11796480 | tf_op jit(solution)/shard_map/all_gather | solution.py:78
  124.1 117.6 %all-gather.11.cloned.1.call-start = ((), (), s32[]{:S(2)}) async-start(), calls=%async_computation.9 | async-start | bytes 11796480 | tf_op jit(solution)/shard_map/all_gather | solution.py:79
  186.5 147.9 %reduce-scatter.7.cloned.1.call-start = ((), (), s32[]{:S(2)}) async-start(), calls=%async_computation.10 | async-start | bytes 8355840
  214.2 5.6 %copy-start.3 = (bf16[16,40,6144]{2,1,0:T(8,128)(2,1)S(1)}, bf16[16,40,6144]{2,1,0:T(8,128)(2,1)}, u32[]{:S(2)}) copy-start(bf16[16,40,6144]{2,1,0:T(8,128)(2,1)} %all-gather.7.cloned.1.call-done) | copy-start | bytes 23592964
  214.2 6.4 %copy-start.6 = (bf16[1,6144,256]{2,1,0:T(8,128)(2,1)S(1)}, bf16[1,6144,256]{2,1,0:T(8,128)(2,1)}, u32[]{:S(2)}) copy-start(bf16[1,6144,256]{2,1,0:T(8,128)(2,1)} %param.16) | copy-start | bytes 9437188
  220.6 3.0 copy-start.7
  220.6 3.8 copy-start.1
  223.6 0.7 copy-start.2
  241.2 110.2 %reduce-scatter.5.cloned.1.call-start = ((), (), s32[]{:S(2)}) async-start(), calls=%async_computation.7 | async-start | bytes 737280 | tf_op jit(solution)/shard_map/reduce_scatter | solution.py:96
  241.6 6.5 %copy-start.5 = (bf16[1,6144,256]{2,1,0:T(8,128)(2,1)S(1)}, bf16[1,6144,256]{2,1,0:T(8,128)(2,1)}, u32[]{:S(2)}) copy-start(bf16[1,6144,256]{2,1,0:T(8,128)(2,1)} %param.15) | copy-start | bytes 9437188
  241.6 6.5 %copy-start.8 = (f32[640,256]{1,0:T(8,128)S(1)}, f32[640,256]{1,0:T(8,128)}, u32[]{:S(2)}) copy-start(f32[640,256]{1,0:T(8,128)} %copy-done.7) | copy-start | bytes 1966084
  241.6 6.5 %copy-start.10 = (f32[640,256]{1,0:T(8,128)S(1)}, f32[640,256]{1,0:T(8,128)}, u32[]{:S(2)}) copy-start(f32[640,256]{1,0:T(8,128)} %get-tuple-element.5) | copy-start | bytes 1966084
  247.2 0.8 copy-start.9
  351.5 18.3 %all-to-all-start.1 = ((bf16[384,8,40]{0,2,1:T(8,128)(2,1)}), bf16[384,8,40]{0,2,1:T(8,128)(2,1)S(1)}, u32[]{:S(2)}, u32[]{:S(2)}) async-start(bf16[384,8,40]{0,2,1:T(8,128)(2,1)} %bitcast.58), calls=%async_computation.2 | async-start | bytes 491520 | tf_op jit(solution)/shard_map/all_to_all | solution.py:101
Sparse Core Ops, SparseCore 0:
  64.9 59.1 all-gather.4
  126.4 59.9 all-gather.8
  188.3 25.9 all-gather.6
  215.9 25.6 all-gather.10
  245.3 89.1 reduce-scatter.6
  336.8 14.6 reduce-scatter.4
where the time goes:
time: 379 us
  waiting for transfers between devices  193 us (51%)
  blocking collectives  96.5 us (25%)
  matrix products  43.9 us (12%)
  local copies, waits for them, and re-layouts  16.8 us (4%)
  between operations  14.2 us (4%)
  other arithmetic  7.42 us (2%)
  starting transfers between devices  6.89 us (2%)
    unnamed x7, waiting for transfers between devices  80.2 us
    all_gather x1, waiting for transfers between devices, on_device(): lax.all_gather(came_cot, 'tp', axis=2, tiled=True)  62.4 us
    psum x1, blocking collectives, on_device(): squares = lax.psum(jnp.sum(wide_hidden * wide_hidden, axis=1), 'tp')  34.2 us
    psum x1, blocking collectives, on_device(): doc_len = lax.psum(jnp.sum(doc_onehot, axis=0), ('tok', 'grp'))  32.2 us
    all_gather x1, waiting for transfers between devices, on_device(): lax.all_gather(part_rows, 'grp', axis=0, tiled=True)  27.7 us
    all_to_all x1, blocking collectives, on_device(): lax.all_to_all(block_rows, 'tok', split_axis=0, concat_axis=0, tiled=True)  17.2 us
    unnamed x25, local copies, waits for them, and re-layouts  16.1 us
    all_to_all x1, blocking collectives, on_device(): lax.all_to_all(block_cot, 'tok', split_axis=0, concat_axis=0, tiled=True)  12.8 us
  transfers between devices with their start and end apart: 7, of which 7 were waited for; matrix products, arithmetic and copies ran while one was open for 15% of the time, Pallas kernels for 0%

commit v1 on v0

--- a/solution.py
+++ b/solution.py
@@ -41,7 +41,8 @@
     width = w_gate.shape[1]
     documents = jnp.arange(experts * groups, dtype=jnp.int32)
     doc_onehot = (segment_ids[:, None] == documents[None, :]).astype(jnp.float32)
-    doc_len = lax.psum(jnp.sum(doc_onehot, axis=0), ("tok", "grp"))
+    body = jnp.sum(doc_onehot, axis=0)
+    doc_len = jax.lax.all_gather(body, axis_name=("tok", "grp")).sum(axis=0)
     tok_len = jnp.sum(doc_onehot * doc_len[None, :], axis=1)
     tok_weight = rows_here / tok_len
     onehot = (

time: 379 us -> 379 us (level)
  waiting for transfers between devices: 193 us -> 188 us
    unnamed x0 -> x1, blocking collectives: none -> 32.6 us
    psum x1 -> x0, blocking collectives: 32.2 us -> none  [on_device(): doc_len = lax.psum(jnp.sum(doc_onehot, axis=0), ('tok', 'grp'))]
    all_gather x1, waiting for transfers between devices: 10.2 us -> 5.28 us  [on_device(): lax.all_gather(came_rows, 'tp', axis=2, tiled=True)]
    unnamed x25 -> x28, local copies, waits for them, and re-layouts: 16.1 us -> 17.6 us
where the time goes in v1:
time: 379 us
  waiting for transfers between devices  188 us (50%)
  blocking collectives  99.2 us (26%)
  matrix products  43.9 us (12%)
  local copies, waits for them, and re-layouts  18.3 us (5%)
  between operations  14.9 us (4%)
  other arithmetic  7.45 us (2%)
  starting transfers between devices  6.88 us (2%)
    unnamed x7, waiting for transfers between devices  80.1 us
    all_gather x1, waiting for transfers between devices, on_device(): lax.all_gather(came_cot, 'tp', axis=2, tiled=True)  62.4 us
    psum x1, blocking collectives, on_device(): squares = lax.psum(jnp.sum(wide_hidden * wide_hidden, axis=1), 'tp')  34.2 us
    unnamed x1, blocking collectives  32.6 us
    all_gather x1, waiting for transfers between devices, on_device(): lax.all_gather(part_rows, 'grp', axis=0, tiled=True)  27.7 us
    unnamed x28, local copies, waits for them, and re-layouts  17.6 us
    all_to_all x1, blocking collectives, on_device(): lax.all_to_all(block_rows, 'tok', split_axis=0, concat_axis=0, tiled=True)  17.2 us
    all_to_all x1, blocking collectives, on_device(): lax.all_to_all(block_cot, 'tok', split_axis=0, concat_axis=0, tiled=True)  15.1 us
  transfers between devices with their start and end apart: 7, of which 7 were waited for; matrix products, arithmetic and copies ran while one was open for 15% of the time, Pallas kernels for 0%

profile of v1, /device:TPU:1, one launch (start us, length us, event | category | flops | bytes accessed | tf_op | source)
XLA Modules:
  0.0 378.6 jit_solution(10056331473833084322)
XLA Ops:
  7.2 0.9 copy.31
  8.2 0.1 eq.56
  8.3 0.1 eq.52
  8.5 1.0 fusion.19
  9.5 34.2 %psum.7 = f32[128]{0:T(128)S(1)} all-reduce(f32[128]{0:T(128)S(1)} %fusion.19), channel_id=1, replica_groups=mesh['tok'=8,'tp'=16,'grp'=2] {'tp'}, use_global_device_ids=true, to_apply=%region_6.7 | all-reduce | flops 128 | bytes 1024 | tf_op jit(solution)/shard_map/psum | solution.py:61
  43.7 0.7 convert_element_type.60
  44.4 0.6 reduce-window.6
  45.0 0.2 slice_reduce_fusion
  45.2 0.1 fusion.27
  45.3 0.1 reshape.79
  45.5 0.1 copy.33
  45.5 0.7 multiply_add_fusion
  46.3 1.2 convolution_convert_fusion.1
  47.5 17.2 %all_to_all.15 = bf16[8,40,384]{2,1,0:T(8,128)(2,1)} all-to-all(bf16[8,40,384]{2,1,0:T(8,128)(2,1)S(1)} %bitcast.57), channel_id=1, replica_groups=mesh['tok'=8,'tp'=16,'grp'=2] {'tok'}, dimensions={0} | all-to-all | bytes 491520 | tf_op jit(solution)/shard_map/all_to_all | solution.py:71
  64.7 0.0 all-gather.10.cloned.1.call-start
  64.8 1.3 dynamic-slice
  66.7 0.8 convert_reduce_fusion
  67.5 0.2 dynamic-update-slice
  67.7 32.6 %all-reduce = f32[256]{0:T(256)S(1)} all-reduce(f32[256]{0:T(256)S(1)} %dynamic-update-slice), channel_id=2, replica_groups=mesh['tok'=8,'tp'=16,'grp'=2] {'tok','grp'}, use_global_device_ids=true, to_apply=%add | all-reduce | flops 256 | bytes 2048
  100.3 0.1 reshape.86
  100.4 0.7 select_reduce_fusion.2
  101.2 0.7 broadcast_multiply_fusion
  101.9 1.5 select_reduce_fusion
  103.4 0.2 fusion.14
  103.6 15.1 %all_to_all.16 = bf16[8,40,384]{2,1,0:T(8,128)(2,1)} all-to-all(bf16[8,40,384]{2,1,0:T(8,128)(2,1)S(1)} %bitcast.58), channel_id=1, replica_groups=mesh['tok'=8,'tp'=16,'grp'=2] {'tok'}, dimensions={0} | all-to-all | bytes 491520 | tf_op jit(solution)/shard_map/all_to_all | solution.py:72
  118.8 5.3 %all-gather.6.cloned.1.call-done = bf16[8,40,6144]{2,1,0:T(8,128)(2,1)} async-done(((bf16[8,40,384]{2,1,0:T(8,128)(2,1)}), bf16[8,40,6144]{2,1,0:T(8,128)(2,1)}) %all-gather.6.cloned.1.call-update) | async-done | bytes 3932176 | tf_op jit(solution)/shard_map/all_gather | solution.py:75
  124.1 62.4 %all-gather.10.cloned.1.call-done = bf16[8,40,6144]{2,1,0:T(8,128)(2,1)} async-done(((bf16[8,40,384]{2,1,0:T(8,128)(2,1)}), bf16[8,40,6144]{2,1,0:T(8,128)(2,1)}) %all-gather.10.cloned.1.call-update) | async-done | bytes 3932176 | tf_op jit(solution)/shard_map/all_gather | solution.py:76
  186.5 27.7 %all-gather.8.cloned.1.call-done = bf16[16,40,6144]{2,1,0:T(8,128)(2,1)} async-done(((bf16[8,40,6144]{2,1,0:T(8,128)(2,1)}), bf16[16,40,6144]{2,1,0:T(8,128)(2,1)}) %all-gather.8.cloned.1.call-update) | async-done | bytes 7864336 | tf_op jit(solution)/shard_map/all_gather | solution.py:79
  214.2 5.6 %fusion.9 = f32[640,256]{1,0:T(8,128)S(1)} fusion(bf16[640,6144]{1,0:T(8,128)(2,1)} %bitcast.61, bf16[1,6144,256]{2,1,0:T(8,128)(2,1)S(1)} %copy-done.4), kind=kOutput, calls=%fused_computation.13 | convolution fusion | flops 2013265920 | bytes 11665408 | tf_op jit(solution)/shard_map/dot_general | solution.py:8
  219.8 0.8 copy-done.6
  220.6 3.0 multiply_convert_fusion.2
  223.6 0.7 copy-done.2
  224.4 6.1 %fusion = bf16[6144,640]{0,1:T(8,128)(2,1)} fusion(bf16[640,256]{1,0:T(8,128)(2,1)S(1)} %get-tuple-element.4, bf16[1,256,6144]{2,1,0:T(8,128)(2,1)S(1)} %copy-done.1), kind=kOutput, calls=%fused_computation.1 | convolution fusion | flops 2017198080 | bytes 11337728 | tf_op jit(solution)/shard_map/dot_general | solution.py:90
  230.5 10.7 %copy.34 = bf16[6144,640]{1,0:T(8,128)(2,1)} copy(bf16[6144,640]{0,1:T(8,128)(2,1)} %fusion) | data formatting | bytes 15728640
  241.2 0.2 reduce-scatter.5.cloned.1.call-start
  241.5 0.1 all-gather.12.cloned.1.call-done
  241.6 5.6 %fusion.4 = f32[640,256]{1,0:T(8,128)S(1)} fusion(bf16[640,6144]{1,0:T(8,128)(2,1)} %bitcast.54, bf16[1,256,6144]{2,1,0:T(8,128)(2,1)S(1)} %copy-done.1), kind=kOutput, calls=%fused_computation.8 | convolution fusion | flops 2013265920 | bytes 11665408 | tf_op jit(solution)/shard_map/dot_general | solution.py:13
  247.2 0.8 copy-done.9
  248.1 6.2 %fusion.11 = f32[256]{0:T(256)S(1)} fusion(bf16[1,6144,256]{2,1,0:T(8,128)(2,1)S(1)} %copy-done.5, bf16[640,6144]{1,0:T(8,128)(2,1)} %bitcast.62, f32[640,256]{1,0:T(8,128)S(1)} %copy-done.8, f32[640,256]{1,0:T(8,128)S(1)} %fusion.4, f32[640,256]{1,0:T(8,128)S(1)} %copy-done.10), kind=kOutput, calls=%fused_computation.15 | convolution fusion | flops 2021195520 | bytes 12977152 | tf_op jit(solution)/shard_map/dot_general | solution.py:20
  254.3 80.0 %reduce-scatter.7.cloned.1.call-done = bf16[384,640]{1,0:T(8,128)(2,1)} async-done(((bf16[6144,640]{1,0:T(8,128)(2,1)}), bf16[384,640]{1,0:T(8,128)(2,1)}) %reduce-scatter.7.cloned.1.call-update) | async-done | bytes 491536
  334.3 2.0 copy.35
  336.4 7.4 %fusion.12 = f32[256]{0:T(256)S(1)} fusion(bf16[1,6144,256]{2,1,0:T(8,128)(2,1)} %param.16, bf16[640,6144]{1,0:T(8,128)(2,1)} %bitcast.63, f32[640,256]{1,0:T(8,128)} %copy-done.9, f32[640,256]{1,0:T(8,128)} %copy-done.7), kind=kOutput, calls=%fused_computation.16 | convolution fusion | flops 2020540160 | bytes 12321792 | tf_op jit(solution)/shard_map/dot_general | solution.py:23
  343.7 7.7 %reduce-scatter.5.cloned.1.call-done = bf16[384,320]{0,1:T(8,128)(2,1)} async-done(((bf16[384,640]{0,1:T(8,128)(2,1)}), bf16[384,320]{0,1:T(8,128)(2,1)}) %reduce-scatter.5.cloned.1.call-update) | async-done | bytes 245776 | tf_op jit(solution)/shard_map/reduce_scatter | solution.py:97
  351.4 6.5 %all-to-all-start.1 = ((bf16[384,8,40]{0,2,1:T(8,128)(2,1)}), bf16[384,8,40]{0,2,1:T(8,128)(2,1)S(1)}, u32[]{:S(2)}, u32[]{:S(2)}) async-start(bf16[384,8,40]{0,2,1:T(8,128)(2,1)} %bitcast.59), calls=%async_computation.2 | async-start | bytes 491520 | tf_op jit(solution)/shard_map/all_to_all | solution.py:102
  357.8 6.5 %fusion.13 = f32[256]{0:T(256)S(1)} fusion(bf16[1,256,6144]{2,1,0:T(8,128)(2,1)S(1)} %copy-done.1, bf16[640,256]{1,0:T(8,128)(2,1)} %copy-done.2, bf16[640,6144]{1,0:T(8,128)(2,1)} %bitcast.55), kind=kOutput, calls=%fused_computation.17 | convolution fusion | flops 2019557120 | bytes 11338752 | tf_op jit(solution)/shard_map/dot_general | solution.py:26
  364.3 0.6 add_multiply_fusion
  364.9 4.8 %all-to-all-done.1 = bf16[384,8,40]{0,2,1:T(8,128)(2,1)S(1)} async-done(((bf16[384,8,40]{0,2,1:T(8,128)(2,1)}), bf16[384,8,40]{0,2,1:T(8,128)(2,1)S(1)}, u32[]{:S(2)}, u32[]{:S(2)}) %all-to-all-start.1) | async-done | bytes 245792 | tf_op jit(solution)/shard_map/all_to_all | solution.py:102
  369.7 2.0 fusion.15
  (37 shorter events, 0.4 us)
Async XLA Ops:
  7.2 96.2 %copy-start = (bf16[128,384]{1,0:T(8,128)(2,1)S(1)}, bf16[128,384]{1,0:T(8,128)(2,1)}, u32[]{:S(2)}) copy-start(bf16[128,384]{1,0:T(8,128)(2,1)} %param.14) | copy-start | bytes 294916
  7.2 207.0 %copy-start.4 = (bf16[1,6144,256]{2,1,0:T(8,128)(2,1)S(1)}, bf16[1,6144,256]{2,1,0:T(8,128)(2,1)}, u32[]{:S(2)}) copy-start(bf16[1,6144,256]{2,1,0:T(8,128)(2,1)} %param.15) | copy-start | bytes 9437188
  7.2 116.8 %all-gather.6.cloned.1.call-start = ((), (), s32[]{:S(2)}) async-start(), calls=%async_computation.5 | async-start | bytes 4177920 | tf_op jit(solution)/shard_map/all_gather | solution.py:75
  64.7 121.7 %all-gather.10.cloned.1.call-start = ((), (), s32[]{:S(2)}) async-start(), calls=%async_computation.8 | async-start | bytes 4177920 | tf_op jit(solution)/shard_map/all_gather | solution.py:76
  118.7 95.5 %all-gather.8.cloned.1.call-start = ((), (), s32[]{:S(2)}) async-start(), calls=%async_computation.6 | async-start | bytes 11796480 | tf_op jit(solution)/shard_map/all_gather | solution.py:79
  124.1 117.6 %all-gather.12.cloned.1.call-start = ((), (), s32[]{:S(2)}) async-start(), calls=%async_computation.9 | async-start | bytes 11796480 | tf_op jit(solution)/shard_map/all_gather | solution.py:80
  186.5 147.8 %reduce-scatter.7.cloned.1.call-start = ((), (), s32[]{:S(2)}) async-start(), calls=%async_computation.10 | async-start | bytes 8355840
  214.2 5.6 %copy-start.3 = (bf16[16,40,6144]{2,1,0:T(8,128)(2,1)S(1)}, bf16[16,40,6144]{2,1,0:T(8,128)(2,1)}, u32[]{:S(2)}) copy-start(bf16[16,40,6144]{2,1,0:T(8,128)(2,1)} %all-gather.8.cloned.1.call-done) | copy-start | bytes 23592964
  214.2 6.4 %copy-start.6 = (bf16[1,6144,256]{2,1,0:T(8,128)(2,1)S(1)}, bf16[1,6144,256]{2,1,0:T(8,128)(2,1)}, u32[]{:S(2)}) copy-start(bf16[1,6144,256]{2,1,0:T(8,128)(2,1)} %param.16) | copy-start | bytes 9437188
  220.6 3.0 copy-start.7
  220.6 3.8 copy-start.1
  223.6 0.7 copy-start.2
  241.2 110.1 %reduce-scatter.5.cloned.1.call-start = ((), (), s32[]{:S(2)}) async-start(), calls=%async_computation.7 | async-start | bytes 737280 | tf_op jit(solution)/shard_map/reduce_scatter | solution.py:97
  241.6 6.5 %copy-start.5 = (bf16[1,6144,256]{2,1,0:T(8,128)(2,1)S(1)}, bf16[1,6144,256]{2,1,0:T(8,128)(2,1)}, u32[]{:S(2)}) copy-start(bf16[1,6144,256]{2,1,0:T(8,128)(2,1)} %param.15) | copy-start | bytes 9437188
  241.6 6.5 %copy-start.8 = (f32[640,256]{1,0:T(8,128)S(1)}, f32[640,256]{1,0:T(8,128)}, u32[]{:S(2)}) copy-start(f32[640,256]{1,0:T(8,128)} %copy-done.7) | copy-start | bytes 1966084
  241.6 6.5 %copy-start.10 = (f32[640,256]{1,0:T(8,128)S(1)}, f32[640,256]{1,0:T(8,128)}, u32[]{:S(2)}) copy-start(f32[640,256]{1,0:T(8,128)} %get-tuple-element.5) | copy-start | bytes 1966084
  247.2 0.8 copy-start.9
  351.4 18.3 %all-to-all-start.1 = ((bf16[384,8,40]{0,2,1:T(8,128)(2,1)}), bf16[384,8,40]{0,2,1:T(8,128)(2,1)S(1)}, u32[]{:S(2)}, u32[]{:S(2)}) async-start(bf16[384,8,40]{0,2,1:T(8,128)(2,1)} %bitcast.59), calls=%async_computation.2 | async-start | bytes 491520 | tf_op jit(solution)/shard_map/all_to_all | solution.py:102
Sparse Core Ops, SparseCore 0:
  64.9 59.1 all-gather.5
  126.4 59.9 all-gather.9
  188.3 25.9 all-gather.7
  215.9 25.6 all-gather.11
  245.3 89.0 reduce-scatter.6
  336.7 14.6 reduce-scatter.4
